TPU v7x, 256 devices: a whole 4x4x8 slice. The times are simulated.
256 devices in a mesh: seq: 8 (over z_lo, x), tensor: 32 (over z_hi, y, core).
Axes of the slice: x: 4, y: 4, z: 8 (z_hi: 4, z_lo: 2; z = z_hi * 2 + z_lo), core: 2. Of those that a mesh axis runs over, the one named last changes fastest.
Arguments:
- tokens: bfloat16 [768, 8192], P('tensor', 'seq'), may hold values from -6 to 6
- w_gate: bfloat16 [8192, 28672], P('seq', 'tensor'), may hold values from -0.109375 to 0.109375
- w_up: bfloat16 [8192, 28672], P('seq', 'tensor'), may hold values from -0.109375 to 0.109375
- w_down: bfloat16 [28672, 8192], P('tensor', 'seq'), may hold values from -0.0546875 to 0.0546875
- mask_gate: int32 [64, 224], P('seq', 'tensor'), may hold values 0 or 1
- mask_up: int32 [64, 224], P('seq', 'tensor'), may hold values 0 or 1
- mask_down: int32 [224, 64], P('tensor', 'seq'), may hold values 0 or 1
- cotangent: bfloat16 [768, 8192], P('tensor', 'seq'), may hold values from -6 to 6
Outputs:
- output: bfloat16 [768, 8192], P('tensor', 'seq')
- grad_tokens: bfloat16 [768, 8192], P('tensor', 'seq')
- grad_gate: bfloat16 [8192, 28672], P('seq', 'tensor')
- grad_up: bfloat16 [8192, 28672], P('seq', 'tensor')
- grad_down: bfloat16 [28672, 8192], P('tensor', 'seq')
All inputs are finite; a program needn't handle non-finite values. No bound on the sum of `mask_gate` or of `mask_up` or of `mask_down` on one device may be relied on, other than what follows from the above.
Results may differ from a plain program's by a relative error of at most 0.0049.
Values may be sent and summed in bfloat16 or wider, within the bound.
A program may use at most 128 MiB of HBM per device.

v0:
```python
import jax
import jax.numpy as jnp
from jax import lax
from jax.sharding import PartitionSpec as P


def widen(mask, rows):
    block = rows // mask.shape[0]
    full = jnp.repeat(jnp.repeat(mask, block, axis=0), block, axis=1)
    return full.astype(jnp.bfloat16)


def gating(summed, width):
    gate = summed[:, :width]
    up = summed[:, width:]
    sig = jax.nn.sigmoid(gate)
    act = gate * sig
    return (gate, up, sig, act)


def gate_up_grads(gate, up, sig, act, grad_hidden):
    dgate = (grad_hidden * up * sig * (1.0 + gate * (1.0 - sig))).astype(jnp.bfloat16)
    dup = (grad_hidden * act).astype(jnp.bfloat16)
    return jnp.concatenate([dgate, dup], axis=1)


def per_device(tokens, w_gate, w_up, w_down, mask_gate, mask_up, mask_down, cotangent):
    width = w_gate.shape[1]
    feat = tokens.shape[1]
    gate_mask = widen(mask_gate, w_gate.shape[0])
    up_mask = widen(mask_up, w_up.shape[0])
    down_mask = widen(mask_down, w_down.shape[0])
    joined = jnp.concatenate([w_gate * gate_mask, w_up * up_mask], axis=1)
    down_w = w_down * down_mask
    contract_first = (((0,), (0,)), ((), ()))
    contract_last = (((1,), (1,)), ((), ()))
    both = lax.all_gather(
        jnp.concatenate([tokens, cotangent], axis=1), "tensor", axis=0, tiled=True
    )
    gathered = both[:, :feat]
    cot_rows = both[:, feat:]
    partial_value = jnp.dot(gathered, joined, preferred_element_type=jnp.float32)
    summed = lax.psum_scatter(partial_value, "seq", scatter_dimension=0, tiled=True)
    gate, up, sig, act = gating(summed, width)
    hidden_part = (act * up).astype(jnp.bfloat16)
    hidden = lax.all_gather(hidden_part, "seq", axis=0, tiled=True)
    output = lax.psum_scatter(
        jnp.dot(hidden, down_w, preferred_element_type=jnp.float32),
        "tensor",
        scatter_dimension=0,
        tiled=True,
    ).astype(jnp.bfloat16)
    grad_part = lax.dot_general(cot_rows, down_w, contract_last, preferred_element_type=jnp.float32)
    grad_hidden = lax.psum_scatter(grad_part, "seq", scatter_dimension=0, tiled=True)
    grads_part = gate_up_grads(gate, up, sig, act, grad_hidden)
    grads = lax.all_gather(grads_part, "seq", axis=0, tiled=True)
    grad_tokens = lax.psum_scatter(
        lax.dot_general(grads, joined, contract_last, preferred_element_type=jnp.float32),
        "tensor",
        scatter_dimension=0,
        tiled=True,
    ).astype(jnp.bfloat16)
    weight_grad = lax.dot_general(
        gathered, grads, contract_first, preferred_element_type=jnp.float32
    )
    grad_gate = (weight_grad[:, :width] * gate_mask).astype(jnp.bfloat16)
    grad_up = (weight_grad[:, width:] * up_mask).astype(jnp.bfloat16)
    down_grad = lax.dot_general(
        hidden, cot_rows, contract_first, preferred_element_type=jnp.float32
    )
    grad_down = (down_grad * down_mask).astype(jnp.bfloat16)
    return (output, grad_tokens, grad_gate, grad_up, grad_down)


def solution(mesh):
    return jax.shard_map(
        per_device,
        mesh=mesh,
        in_specs=(
            P("tensor", "seq"),
            P("seq", "tensor"),
            P("seq", "tensor"),
            P("tensor", "seq"),
            P("seq", "tensor"),
            P("seq", "tensor"),
            P("tensor", "seq"),
            P("tensor", "seq"),
        ),
        out_specs=(
            P("tensor", "seq"),
            P("tensor", "seq"),
            P("seq", "tensor"),
            P("seq", "tensor"),
            P("tensor", "seq"),
        ),
        check_vma=False,
    )
```

profile of v0, /device:TPU:2, one launch (start us, length us, event | category | flops | bytes accessed | tf_op | source)
XLA Modules:
  0.0 488.6 jit_solution(1921421634901228654)
XLA Ops:
  7.2 1.6 pad_maximum_fusion.4
  8.9 0.7 convert_element_type.73
  9.6 61.6 %all-gather.4.cloned.1.call-done = bf16[768,2048]{1,0:T(8,128)(2,1)} async-done(((bf16[24,2048]{1,0:T(8,128)(2,1)}), bf16[768,2048]{1,0:T(8,128)(2,1)}) %all-gather.4.cloned.1.call-update) | async-done | bytes 3145744 | tf_op jit(solution)/shard_map/all_gather | solution.py:37
  71.2 1.1 broadcast_in_dim.23
  72.3 1.2 copy-done.4
  73.5 4.8 fusion.5
  78.4 0.6 copy-done.6
  79.4 2.9 copy.14
  82.3 3.8 copy.16
  86.1 1.9 bitcast_multiply_fusion.1
  88.1 1.2 copy-done.1
  89.3 0.6 copy-done.3
  89.9 4.8 fusion.3
  94.8 27.1 %reduce-scatter.9.cloned.1.call-done = f32[96,896]{1,0:T(8,128)} async-done(((f32[768,896]{1,0:T(8,128)}), f32[96,896]{1,0:T(8,128)}) %reduce-scatter.9.cloned.1.call-update) | async-done | bytes 344080 | tf_op jit(solution)/shard_map/reduce_scatter | solution.py:54
  121.9 69.5 %reduce-scatter.5.cloned.1.call-done = f32[96,1792]{1,0:T(8,128)} async-done(((f32[768,1792]{1,0:T(8,128)}), f32[96,1792]{1,0:T(8,128)}) %reduce-scatter.5.cloned.1.call-update) | async-done | bytes 688144 | tf_op jit(solution)/shard_map/reduce_scatter | solution.py:43
  191.4 2.0 multiply_convert_fusion.2
  193.5 0.8 pad_maximum_fusion.3
  194.3 40.4 %all-gather.6.cloned.1.call-done = bf16[768,896]{1,0:T(8,128)(2,1)} async-done(((bf16[96,896]{1,0:T(8,128)(2,1)}), bf16[768,896]{1,0:T(8,128)(2,1)}) %all-gather.6.cloned.1.call-update) | async-done | bytes 1376272 | tf_op jit(solution)/shard_map/all_gather | solution.py:46
  234.7 5.5 %fusion.10 = f32[768,1024]{1,0:T(8,128)} fusion(bf16[768,896]{1,0:T(8,128)(2,1)} %all-gather.6.cloned.1.call-done, bf16[896,1024]{1,0:T(8,128)(2,1)} %param.11, bf16[112,8,8,128]{3,2,1,0:T(8,128)(2,1)S(1)} %bitcast.33), kind=kOutput, calls=%fused_computation.17 | convolution fusion | flops 1410203648 | bytes 8192000 | tf_op jit(solution)/shard_map/dot_general | solution.py:48
  240.5 41.6 %all-gather.8.cloned.1.call-done = bf16[768,1792]{1,0:T(8,128)(2,1)} async-done(((bf16[96,1792]{1,0:T(8,128)(2,1)}), bf16[768,1792]{1,0:T(8,128)(2,1)}) %all-gather.8.cloned.1.call-update) | async-done | bytes 2752528 | tf_op jit(solution)/shard_map/all_gather | solution.py:56
  282.1 7.1 %fusion.2 = f32[768,1024]{1,0:T(8,128)} fusion(bf16[768,1792]{1,0:T(8,128)(2,1)} %all-gather.8.cloned.1.call-done, bf16[1024,896]{0,1:T(8,128)(2,1)S(1)} %copy-done.2, bf16[1024,896]{0,1:T(8,128)(2,1)} %copy-done.3), kind=kOutput, calls=%fused_computation.6 | convolution fusion | flops 2825912320 | bytes 9568256 | tf_op jit(solution)/shard_map/dot_general | solution.py:58
  289.2 1.5 broadcast_in_dim.19
  290.7 3.1 copy.17
  293.7 1.5 broadcast_in_dim.21
  295.2 3.9 copy.18
  299.1 5.0 %multiply_convert_fusion = bf16[896,1024]{1,0:T(8,128)(2,1)} fusion(bf16[768,896]{1,0:T(8,128)(2,1)S(1)} %copy-done.12, bf16[112,8,8,128]{3,2,1,0:T(8,128)(2,1)} %bitcast.32, bf16[768,2048]{1,0:T(8,128)(2,1)} %all-gather.4.cloned.1.call-done), kind=kOutput, calls=%fused_computation.5 | convolution fusion | flops 1412038656 | bytes 6619136 | tf_op jit(solution)/shard_map/dot_general | solution.py:68
  304.2 3.1 fusion.7
  307.3 2.8 fusion
  310.1 73.0 %reduce-scatter.7.cloned.1.call-done = f32[24,1024]{1,0:T(8,128)} async-done(((f32[768,1024]{1,0:T(8,128)}), f32[24,1024]{1,0:T(8,128)}) %reduce-scatter.7.cloned.1.call-update) | async-done | bytes 98320 | tf_op jit(solution)/shard_map/reduce_scatter | solution.py:47
  383.1 1.5 convert_element_type.76
  384.6 95.6 %reduce-scatter.11.cloned.1.call-done = f32[24,1024]{1,0:T(8,128)} async-done(((f32[768,1024]{1,0:T(8,128)}), f32[24,1024]{1,0:T(8,128)}) %reduce-scatter.11.cloned.1.call-update) | async-done | bytes 98320 | tf_op jit(solution)/shard_map/reduce_scatter | solution.py:57
  480.2 1.5 convert_element_type.79
  (45 shorter events, 1.0 us)
Async XLA Ops:
  7.2 66.4 %copy-start.11 = (bf16[896,1024]{1,0:T(8,128)(2,1)S(1)}, bf16[896,1024]{1,0:T(8,128)(2,1)}, u32[]{:S(2)}) copy-start(bf16[896,1024]{1,0:T(8,128)(2,1)} %param.11) | copy-start | bytes 5505028
  7.2 64.0 %all-gather.4.cloned.1.call-start = ((), (), s32[]{:S(2)}) async-start(), calls=%async_computation.4 | async-start | bytes 3244032 | tf_op jit(solution)/shard_map/all_gather | solution.py:37
  8.8 113.1 %reduce-scatter.9.cloned.1.call-start = ((), (), s32[]{:S(2)}) async-start(), calls=%async_computation.8 | async-start | bytes 3096576 | tf_op jit(solution)/shard_map/reduce_scatter | solution.py:54
  72.3 1.2 copy-start.4
  78.3 0.7 copy-start.6
  78.3 0.9 copy-start.7
  78.4 113.0 %reduce-scatter.5.cloned.1.call-start = ((), (), s32[]{:S(2)}) async-start(), calls=%async_computation.5 | async-start | bytes 6193152 | tf_op jit(solution)/shard_map/reduce_scatter | solution.py:43
  86.1 3.8 copy-start.8
  88.1 1.2 copy-start.1
  88.1 1.8 copy-start.3
  94.7 140.0 %copy-start.5 = (bf16[896,8,128]{2,1,0:T(8,128)(2,1)S(1)}, bf16[896,8,128]{2,1,0:T(8,128)(2,1)}, u32[]{:S(2)}) copy-start(bf16[896,8,128]{2,1,0:T(8,128)(2,1)} %copy-done.4) | copy-start | bytes 5505028
  94.7 140.0 %all-gather.6.cloned.1.call-start = ((), (), s32[]{:S(2)}) async-start(), calls=%async_computation.6 | async-start | bytes 1548288 | tf_op jit(solution)/shard_map/all_gather | solution.py:46
  193.4 88.7 %all-gather.8.cloned.1.call-start = ((), (), s32[]{:S(2)}) async-start(), calls=%async_computation.9 | async-start | bytes 3096576 | tf_op jit(solution)/shard_map/all_gather | solution.py:56
  194.3 188.8 %reduce-scatter.7.cloned.1.call-start = ((), (), s32[]{:S(2)}) async-start(), calls=%async_computation.7 | async-start | bytes 3244032 | tf_op jit(solution)/shard_map/reduce_scatter | solution.py:47
  240.2 41.9 %copy-start.2 = (bf16[1024,896]{0,1:T(8,128)(2,1)S(1)}, bf16[1024,896]{0,1:T(8,128)(2,1)}, u32[]{:S(2)}) copy-start(bf16[1024,896]{0,1:T(8,128)(2,1)} %copy-done.1) | copy-start | bytes 5505028
  240.2 240.0 %reduce-scatter.11.cloned.1.call-start = ((), (), s32[]{:S(2)}) async-start(), calls=%async_computation.10 | async-start | bytes 3244032 | tf_op jit(solution)/shard_map/reduce_scatter | solution.py:57
  295.2 3.9 copy-start.12
  299.1 5.1 %copy-start.9 = (bf16[768,2048]{1,0:T(8,128)(2,1)S(1)}, bf16[768,2048]{1,0:T(8,128)(2,1)}, u32[]{:S(2)}) copy-start(bf16[768,2048]{1,0:T(8,128)(2,1)} %all-gather.4.cloned.1.call-done) | copy-start | bytes 9437188
  299.1 5.1 %copy-start.10 = (bf16[768,1792]{1,0:T(8,128)(2,1)S(1)}, bf16[768,1792]{1,0:T(8,128)(2,1)}, u32[]{:S(2)}) copy-start(bf16[768,1792]{1,0:T(8,128)(2,1)} %all-gather.8.cloned.1.call-done) | copy-start | bytes 8257540
  304.2 3.1 copy-start
Sparse Core Ops, SparseCore 0:
  11.1 59.9 all-gather.3
  78.5 43.3 reduce-scatter.8
  124.7 66.6 reduce-scatter.4
  193.6 41.1 all-gather.5
  236.5 45.5 all-gather.7
  286.4 96.6 reduce-scatter.6
  387.0 93.1 reduce-scatter.10
where the time goes:
time: 489 us
  waiting for transfers between devices  409 us (84%)
  matrix products  30.3 us (6%)
  local copies, waits for them, and re-layouts  21.8 us (4%)
  between operations  14.3 us (3%)
  other arithmetic  12.8 us (3%)
    reduce_scatter x1, waiting for transfers between devices, per_device(): lax.psum_scatter(lax.dot_general(grads, joined, contract_last, preferred_...  95.6 us
    reduce_scatter x1, waiting for transfers between devices, per_device(): lax.psum_scatter(jnp.dot(hidden, down_w, preferred_element_type=jnp.float...  73 us
    reduce_scatter x1, waiting for transfers between devices, per_device(): lax.psum_scatter(partial_value, 'seq', scatter_dimension=0, tiled=True)  69.5 us
    all_gather x1, waiting for transfers between devices, per_device(): lax.all_gather(jnp.concatenate([tokens, cotangent], axis=1), 'tensor', ax...  61.6 us
    all_gather x1, waiting for transfers between devices, per_device(): grads = lax.all_gather(grads_part, 'seq', axis=0, tiled=True)  41.6 us
    all_gather x1, waiting for transfers between devices, per_device(): hidden = lax.all_gather(hidden_part, 'seq', axis=0, tiled=True)  40.4 us
    reduce_scatter x1, waiting for transfers between devices, per_device(): lax.psum_scatter(grad_part, 'seq', scatter_dimension=0, tiled=True)  27.1 us
    unnamed x32, local copies, waits for them, and re-layouts  10.5 us
  transfers between devices with their start and end apart: 7, of which 7 were waited for; matrix products, arithmetic and copies ran while one was open for 10% of the time, Pallas kernels for 0%

commit v1 on v0

--- a/solution.py
+++ b/solution.py
@@ -43,7 +43,9 @@
     summed = lax.psum_scatter(partial_value, "seq", scatter_dimension=0, tiled=True)
     gate, up, sig, act = gating(summed, width)
     hidden_part = (act * up).astype(jnp.bfloat16)
-    hidden = lax.all_gather(hidden_part, "seq", axis=0, tiled=True)
+    hidden = jnp.concatenate(
+        lax.all_to_all(jnp.stack([hidden_part] * lax.axis_size("seq")), "seq", 0, 0), axis=0
+    )
     output = lax.psum_scatter(
         jnp.dot(hidden, down_w, preferred_element_type=jnp.float32),
         "tensor",

time: 489 us -> 452 us (0.924)
  waiting for transfers between devices: 409 us -> 343 us
  blocking collectives: 0 us -> 31.8 us
    all_gather x1 -> x0, waiting for transfers between devices: 40.4 us -> none  [per_device(): hidden = lax.all_gather(hidden_part, 'seq', axis=0, tiled=True)]
    all_to_all x0 -> x1, blocking collectives: none -> 31.8 us  [per_device(): lax.all_to_all(jnp.stack([hidden_part] * lax.axis_size('seq')), 'seq', 0, 0)]
    all_gather x1, waiting for transfers between devices: 41.6 us -> 16.1 us  [per_device(): grads = lax.all_gather(grads_part, 'seq', axis=0, tiled=True)]
  transfers between devices with their start and end apart: 7 -> 6, of which waited for: 7 -> 6; matrix products, arithmetic and copies ran while one was open for 10% -> 10% of each run, Pallas kernels for 0% -> 0%
where the time goes in v1:
time: 452 us; the launch traced here: 451 us
  waiting for transfers between devices  343 us (76%)
  blocking collectives  31.8 us (7%)
  matrix products  28.2 us (6%)
  local copies, waits for them, and re-layouts  21.8 us (5%)
  between operations  14.3 us (3%)
  other arithmetic  12.2 us (3%)
    reduce_scatter x1, waiting for transfers between devices, per_device(): lax.psum_scatter(lax.dot_general(grads, joined, contract_last, preferred_...  95.5 us
    reduce_scatter x1, waiting for transfers between devices, per_device(): lax.psum_scatter(jnp.dot(hidden, down_w, preferred_element_type=jnp.float...  72.9 us
    reduce_scatter x1, waiting for transfers between devices, per_device(): lax.psum_scatter(partial_value, 'seq', scatter_dimension=0, tiled=True)  69.5 us
    all_gather x1, waiting for transfers between devices, per_device(): lax.all_gather(jnp.concatenate([tokens, cotangent], axis=1), 'tensor', ax...  61.6 us
    all_to_all x1, blocking collectives, per_device(): lax.all_to_all(jnp.stack([hidden_part] * lax.axis_size('seq')), 'seq', 0, 0)  31.8 us
    reduce_scatter x1, waiting for transfers between devices, per_device(): lax.psum_scatter(grad_part, 'seq', scatter_dimension=0, tiled=True)  27.1 us
    all_gather x1, waiting for transfers between devices, per_device(): grads = lax.all_gather(grads_part, 'seq', axis=0, tiled=True)  16.1 us
    unnamed x32, local copies, waits for them, and re-layouts  10.5 us
  transfers between devices with their start and end apart: 6, of which 6 were waited for; matrix products, arithmetic and copies ran while one was open for 10% of the time, Pallas kernels for 0%

profile of v1, /device:TPU:2, one launch (start us, length us, event | category | flops | bytes accessed | tf_op | source)
XLA Modules:
  0.0 451.4 jit_solution(664839781272105210)
XLA Ops:
  7.2 1.6 pad_maximum_fusion.4
  8.9 0.7 convert_element_type.73
  9.6 61.6 %all-gather.3.cloned.1.call-done = bf16[768,2048]{1,0:T(8,128)(2,1)} async-done(((bf16[24,2048]{1,0:T(8,128)(2,1)}), bf16[768,2048]{1,0:T(8,128)(2,1)}) %all-gather.3.cloned.1.call-update) | async-done | bytes 3145744 | tf_op jit(solution)/shard_map/all_gather | solution.py:37
  71.2 1.1 broadcast_in_dim.23
  72.3 1.2 copy-done.4
  73.5 4.8 %fusion.5 = f32[768,896]{1,0:T(8,128)} fusion(bf16[768,2048]{1,0:T(8,128)(2,1)} %all-gather.3.cloned.1.call-done, bf16[896,1024]{1,0:T(8,128)(2,1)S(1)} %copy-done.11, bf16[112,8,8,128]{3,2,1,0:T(8,128)(2,1)S(1)} %bitcast.32), kind=kOutput, calls=%fused_computation.10 | convolution fusion | flops 1410203648 | bytes 7995392 | tf_op jit(solution)/shard_map/dot_general | solution.py:55
  78.4 0.6 copy-done.6
  79.4 2.9 copy.14
  82.3 3.8 copy.16
  86.1 1.9 bitcast_multiply_fusion.1
  88.1 1.2 copy-done.1
  89.3 0.6 copy-done.3
  89.9 4.8 %fusion.3 = f32[768,1792]{1,0:T(8,128)} fusion(bf16[1024,896]{0,1:T(8,128)(2,1)S(1)} %get-tuple-element.10, bf16[1024,896]{0,1:T(8,128)(2,1)S(1)} %get-tuple-element.11, bf16[768,2048]{1,0:T(8,128)(2,1)S(1)} %copy-done.8), kind=kOutput, calls=%fused_computation.7 | convolution fusion | flops 2825912320 | bytes 10747904 | tf_op jit(solution)/shard_map/dot_general | solution.py:42
  94.8 27.1 %reduce-scatter.9.cloned.1.call-done = f32[96,896]{1,0:T(8,128)} async-done(((f32[768,896]{1,0:T(8,128)}), f32[96,896]{1,0:T(8,128)}) %reduce-scatter.9.cloned.1.call-update) | async-done | bytes 344080 | tf_op jit(solution)/shard_map/reduce_scatter | solution.py:56
  121.9 69.5 %reduce-scatter.5.cloned.1.call-done = f32[96,1792]{1,0:T(8,128)} async-done(((f32[768,1792]{1,0:T(8,128)}), f32[96,1792]{1,0:T(8,128)}) %reduce-scatter.5.cloned.1.call-update) | async-done | bytes 688144 | tf_op jit(solution)/shard_map/reduce_scatter | solution.py:43
  191.4 1.4 multiply_convert_fusion.2
  192.8 0.8 pad_maximum_fusion.3
  193.7 31.8 %all_to_all.5 = bf16[8,96,896]{2,1,0:T(8,128)(2,1)S(1)} all-to-all(bf16[8,96,896]{2,1,0:T(8,128)(2,1)S(1)} %stack.2), channel_id=1, replica_groups=mesh['seq'=8,'tensor'=32] {'seq'}, dimensions={0} | all-to-all | bytes 2752512 | tf_op jit(solution)/shard_map/all_to_all | solution.py:47
  225.6 3.5 fusion.10
  229.3 16.1 %all-gather.5.cloned.1.call-done = bf16[768,1792]{1,0:T(8,128)(2,1)} async-done(((bf16[96,1792]{1,0:T(8,128)(2,1)}), bf16[768,1792]{1,0:T(8,128)(2,1)}) %all-gather.5.cloned.1.call-update) | async-done | bytes 2752528 | tf_op jit(solution)/shard_map/all_gather | solution.py:58
  245.4 7.0 %fusion.2 = f32[768,1024]{1,0:T(8,128)} fusion(bf16[768,1792]{1,0:T(8,128)(2,1)} %all-gather.5.cloned.1.call-done, bf16[1024,896]{0,1:T(8,128)(2,1)S(1)} %copy-done.2, bf16[1024,896]{0,1:T(8,128)(2,1)} %copy-done.3), kind=kOutput, calls=%fused_computation.6 | convolution fusion | flops 2825912320 | bytes 9568256 | tf_op jit(solution)/shard_map/dot_general | solution.py:60
  252.4 1.5 broadcast_in_dim.19
  253.8 3.1 copy.17
  256.9 1.5 broadcast_in_dim.21
  258.4 3.8 copy.18
  262.2 5.0 %multiply_convert_fusion = bf16[896,1024]{1,0:T(8,128)(2,1)} fusion(bf16[768,896]{1,0:T(8,128)(2,1)S(1)} %bitcast.36, bf16[112,8,8,128]{3,2,1,0:T(8,128)(2,1)} %bitcast.33, bf16[768,2048]{1,0:T(8,128)(2,1)} %all-gather.3.cloned.1.call-done), kind=kOutput, calls=%fused_computation.5 | convolution fusion | flops 1412038656 | bytes 6619136 | tf_op jit(solution)/shard_map/dot_general | solution.py:70
  267.2 3.1 fusion.7
  270.4 2.8 fusion
  273.1 72.9 %reduce-scatter.7.cloned.1.call-done = f32[24,1024]{1,0:T(8,128)} async-done(((f32[768,1024]{1,0:T(8,128)}), f32[24,1024]{1,0:T(8,128)}) %reduce-scatter.7.cloned.1.call-update) | async-done | bytes 98320 | tf_op jit(solution)/shard_map/reduce_scatter | solution.py:49
  346.0 1.5 convert_element_type.76
  347.5 95.5 %reduce-scatter.11.cloned.1.call-done = f32[24,1024]{1,0:T(8,128)} async-done(((f32[768,1024]{1,0:T(8,128)}), f32[24,1024]{1,0:T(8,128)}) %reduce-scatter.11.cloned.1.call-update) | async-done | bytes 98320 | tf_op jit(solution)/shard_map/reduce_scatter | solution.py:59
  443.0 1.5 convert_element_type.79
  (44 shorter events, 1.1 us)
Async XLA Ops:
  7.2 66.4 %copy-start.11 = (bf16[896,1024]{1,0:T(8,128)(2,1)S(1)}, bf16[896,1024]{1,0:T(8,128)(2,1)}, u32[]{:S(2)}) copy-start(bf16[896,1024]{1,0:T(8,128)(2,1)} %param.11) | copy-start | bytes 5505028
  7.2 64.0 %all-gather.3.cloned.1.call-start = ((), (), s32[]{:S(2)}) async-start(), calls=%async_computation.5 | async-start | bytes 3244032 | tf_op jit(solution)/shard_map/all_gather | solution.py:37
  8.8 113.1 %reduce-scatter.9.cloned.1.call-start = ((), (), s32[]{:S(2)}) async-start(), calls=%async_computation.8 | async-start | bytes 3096576 | tf_op jit(solution)/shard_map/reduce_scatter | solution.py:56
  72.3 1.2 copy-start.4
  78.3 0.7 copy-start.6
  78.3 0.9 copy-start.7
  78.4 113.0 %reduce-scatter.5.cloned.1.call-start = ((), (), s32[]{:S(2)}) async-start(), calls=%async_computation.6 | async-start | bytes 6193152 | tf_op jit(solution)/shard_map/reduce_scatter | solution.py:43
  86.1 3.8 copy-start.8
  88.1 1.2 copy-start.1
  88.1 1.8 copy-start.3
  94.7 150.7 %all-gather.5.cloned.1.call-start = ((), (), s32[]{:S(2)}) async-start(), calls=%async_computation.9 | async-start | bytes 3096576 | tf_op jit(solution)/shard_map/all_gather | solution.py:58
  193.5 152.5 %reduce-scatter.7.cloned.1.call-start = ((), (), s32[]{:S(2)}) async-start(), calls=%async_computation.7 | async-start | bytes 3244032 | tf_op jit(solution)/shard_map/reduce_scatter | solution.py:49
  193.6 32.0 %copy-start.5 = (bf16[896,8,128]{2,1,0:T(8,128)(2,1)S(1)}, bf16[896,8,128]{2,1,0:T(8,128)(2,1)}, u32[]{:S(2)}) copy-start(bf16[896,8,128]{2,1,0:T(8,128)(2,1)} %copy-done.4) | copy-start | bytes 5505028
  193.6 32.0 %copy-start.12 = (bf16[896,1024]{1,0:T(8,128)(2,1)S(1)}, bf16[896,1024]{1,0:T(8,128)(2,1)}, u32[]{:S(2)}) copy-start(bf16[896,1024]{1,0:T(8,128)(2,1)} %param.11) | copy-start | bytes 5505028
  229.1 16.3 %copy-start.2 = (bf16[1024,896]{0,1:T(8,128)(2,1)S(1)}, bf16[1024,896]{0,1:T(8,128)(2,1)}, u32[]{:S(2)}) copy-start(bf16[1024,896]{0,1:T(8,128)(2,1)} %copy-done.1) | copy-start | bytes 5505028
  229.1 213.9 %reduce-scatter.11.cloned.1.call-start = ((), (), s32[]{:S(2)}) async-start(), calls=%async_computation.10 | async-start | bytes 3244032 | tf_op jit(solution)/shard_map/reduce_scatter | solution.py:59
  262.2 5.1 %copy-start.9 = (bf16[768,2048]{1,0:T(8,128)(2,1)S(1)}, bf16[768,2048]{1,0:T(8,128)(2,1)}, u32[]{:S(2)}) copy-start(bf16[768,2048]{1,0:T(8,128)(2,1)} %all-gather.3.cloned.1.call-done) | copy-start | bytes 9437188
  262.2 5.1 %copy-start.10 = (bf16[768,1792]{1,0:T(8,128)(2,1)S(1)}, bf16[768,1792]{1,0:T(8,128)(2,1)}, u32[]{:S(2)}) copy-start(bf16[768,1792]{1,0:T(8,128)(2,1)} %all-gather.5.cloned.1.call-done) | copy-start | bytes 8257540
  267.2 3.1 copy-start
Sparse Core Ops, SparseCore 0:
  11.1 59.9 all-gather.2
  78.5 43.3 reduce-scatter.8
  124.7 66.6 reduce-scatter.4
  193.7 51.6 all-gather.4
  249.7 96.2 reduce-scatter.6
  349.8 93.1 reduce-scatter.10
